TPU v7x, 128 devices: a whole 4x4x4 slice. The times are simulated.
128 devices in a mesh: row: 16 (over y, z), col: 8 (over x, core).
Axes of the slice: x: 4, y: 4, z: 4, core: 2. Of those that a mesh axis runs over, the one named last changes fastest.
Arguments:
- right_side: bfloat16 [8, 16, 8, 128, 512], P(None, 'row', 'col'), may hold values from -6 to 6
- diag_inverse: bfloat16 [8, 16, 8, 128, 128], P(None, 'row', 'col'), may hold values from -1.5 to 1.5, as said below
- factor: bfloat16 [7, 16, 16, 8, 4, 128, 128], P(None, None, 'row', 'col'), may hold values from -0.0625 to 0.0625
- sources: int32 [7, 16, 16, 8, 4], P(None, None, 'row', 'col'), may hold values from 0 to 55, as said below
Outputs:
- solution: float32 [8, 16, 8, 128, 512], P(None, 'row', 'col')
Inputs may be any that keep to these rules, and one draw needn't show every extreme that they name: `diag_inverse`: each block is the inverse of a lower triangular diagonal block of the factor, hence lower triangular. `sources`: for a target of level l (first index l - 1), each entry numbers a solved block of a level below l in the same source grid row r as level * 8 + grid column. The 4 entries of one target, source grid row and target grid column are distinct; the first 2 lie in level l - 1 and the last 2 in levels below l - 1, except for l = 1, where all lie in level 0.
All inputs are finite; a program needn't handle non-finite values.
Results may differ from a plain program's by a relative error of at most 0.008.
Values may be sent and summed in bfloat16 or wider, within the bound.
No kernel may reach another device: no remote copies, remote signals or barrier semaphores. Data moves between devices by JAX's collectives and lax.ppermute only.
A program may use at most 192 MiB of HBM per device.

v0:
```python
import jax
import jax.numpy as jnp
from jax import lax
from jax.sharding import PartitionSpec as P


def broadcast_solved(solved_block):
    return lax.all_gather(solved_block[None], "col", axis=0, tiled=True)


def reduce_updates(update_term):
    return lax.psum_scatter(
        update_term(jnp.int32(0), 1 * lax.axis_size("row")), "row", scatter_dimension=0, tiled=True
    )


def contribute(blocks, source_pool, source_ids):
    picked = jnp.take(source_pool, source_ids, axis=0)
    return jnp.einsum("tkab,tkbn->tan", blocks, picked, preferred_element_type=jnp.float32)


def make_term(blocks, source_pool, source_ids):

    def update_term(first_row, row_count):
        return contribute(blocks, source_pool, source_ids)

    return update_term


def solve_columns(right_side, diag_inverse, factor, sources, col_first, col_last):
    level_total = right_side.shape[0]
    history = []
    solution_list = []
    for level_index in range(level_total):
        own_side = right_side[level_index, 0, 0, :, col_first:col_last]
        if level_index == 0:
            reduced = own_side
        else:
            blocks = factor[level_index - 1, :, 0, 0]
            source_ids = sources[level_index - 1, :, 0, 0, :]
            source_pool = jnp.concatenate(history, axis=0)
            update = reduce_updates(make_term(blocks, source_pool, source_ids))
            reduced = (own_side.astype(jnp.float32) - update[0]).astype(jnp.bfloat16)
        solution = jnp.dot(
            diag_inverse[level_index, 0, 0], reduced, preferred_element_type=jnp.float32
        )
        solution_list.append(solution)
        if level_index + 1 < level_total:
            history.append(broadcast_solved(solution.astype(jnp.bfloat16)))
    return jnp.stack(solution_list)


def per_device(right_side, diag_inverse, factor, sources):
    col_total = right_side.shape[-1]
    solution = solve_columns(right_side, diag_inverse, factor, sources, 0, col_total)
    return solution[:, None, None]


def solution(mesh):
    placed = (
        P(None, "row", "col", None, None),
        P(None, "row", "col", None, None),
        P(None, None, "row", "col", None, None, None),
        P(None, None, "row", "col", None),
    )
    return jax.shard_map(
        per_device,
        mesh=mesh,
        in_specs=placed,
        out_specs=P(None, "row", "col", None, None),
        check_vma=False,
    )
```

profile of v0, /device:TPU:0, one launch (start us, length us, event | category | flops | bytes accessed | tf_op | source)
XLA Modules:
  0.0 952.0 jit_solution(17876641875087454846)
XLA Ops:
  11.5 23.3 %all-gather.15.cloned.1.call-done = bf16[1024,512]{1,0:T(8,128)(2,1)} async-done(((bf16[128,512]{1,0:T(8,128)(2,1)}), bf16[1024,512]{1,0:T(8,128)(2,1)}) %all-gather.15.cloned.1.call-update) | async-done | bytes 1048592 | tf_op jit(solution)/shard_map/all_gather | solution.py:8
  34.8 6.7 gather_fusion
  41.5 12.0 %copy.94 = bf16[64,128,512]{1,2,0:T(8,128)(2,1)} copy(bf16[64,128,512]{2,1,0:T(8,128)(2,1)} %gather_fusion) | data formatting | bytes 16777216 | tf_op jit(solution)/shard_map/jit(_take)/gather | solution.py:18
  53.5 8.5 fusion.28
  63.0 77.8 %reduce-scatter.22.cloned.1.call-done = f32[1,128,512]{1,2,0:T(8,128)} async-done(((f32[16,128,512]{1,2,0:T(8,128)}), f32[1,128,512]{1,2,0:T(8,128)}) %reduce-scatter.22.cloned.1.call-update) | async-done | bytes 262160
  143.6 21.5 %all-gather.17.cloned.1.call-done = bf16[1024,512]{1,0:T(8,128)(2,1)} async-done(((bf16[128,512]{1,0:T(8,128)(2,1)}), bf16[1024,512]{1,0:T(8,128)(2,1)}) %all-gather.17.cloned.1.call-update) | async-done | bytes 1048592 | tf_op jit(solution)/shard_map/all_gather | solution.py:8
  166.5 5.5 gather_fusion.1
  172.1 12.0 %copy.100 = bf16[64,128,512]{1,2,0:T(8,128)(2,1)} copy(bf16[64,128,512]{2,1,0:T(8,128)(2,1)} %gather_fusion.1) | data formatting | bytes 16777216 | tf_op jit(solution)/shard_map/jit(_take)/gather | solution.py:18
  184.1 8.5 fusion.31
  192.8 78.5 %reduce-scatter.24.cloned.1.call-done = f32[1,128,512]{1,2,0:T(8,128)} async-done(((f32[16,128,512]{1,2,0:T(8,128)}), f32[1,128,512]{1,2,0:T(8,128)}) %reduce-scatter.24.cloned.1.call-update) | async-done | bytes 262160
  271.3 1.9 bitcast_dynamic-update-slice_fusion.4
  274.1 21.5 %all-gather.19.cloned.1.call-done = bf16[1024,512]{1,0:T(8,128)(2,1)} async-done(((bf16[128,512]{1,0:T(8,128)(2,1)}), bf16[1024,512]{1,0:T(8,128)(2,1)}) %all-gather.19.cloned.1.call-update) | async-done | bytes 1048592 | tf_op jit(solution)/shard_map/all_gather | solution.py:8
  295.6 2.9 pad_maximum_fusion.1
  298.5 7.4 gather_fusion.2
  305.9 12.0 %copy.106 = bf16[64,128,512]{1,2,0:T(8,128)(2,1)} copy(bf16[64,128,512]{2,1,0:T(8,128)(2,1)} %gather_fusion.2) | data formatting | bytes 16777216 | tf_op jit(solution)/shard_map/jit(_take)/gather | solution.py:18
  317.9 8.5 fusion.34
  328.2 77.0 %reduce-scatter.26.cloned.1.call-done = f32[1,128,512]{1,2,0:T(8,128)} async-done(((f32[16,128,512]{1,2,0:T(8,128)}), f32[1,128,512]{1,2,0:T(8,128)}) %reduce-scatter.26.cloned.1.call-update) | async-done | bytes 262160
  405.2 2.0 bitcast_dynamic-update-slice_fusion.3
  410.1 19.5 %all-gather.21.cloned.1.call-done = bf16[1024,512]{1,0:T(8,128)(2,1)} async-done(((bf16[128,512]{1,0:T(8,128)(2,1)}), bf16[1024,512]{1,0:T(8,128)(2,1)}) %all-gather.21.cloned.1.call-update) | async-done | bytes 1048592 | tf_op jit(solution)/shard_map/all_gather | solution.py:8
  429.6 3.4 pad_maximum_fusion
  433.0 7.8 gather_fusion.3
  440.8 11.9 %copy.112 = bf16[64,128,512]{1,2,0:T(8,128)(2,1)} copy(bf16[64,128,512]{2,1,0:T(8,128)(2,1)} %gather_fusion.3) | data formatting | bytes 16777216 | tf_op jit(solution)/shard_map/jit(_take)/gather | solution.py:18
  452.7 8.3 fusion.37
  462.7 77.0 %reduce-scatter.28.cloned.1.call-done = f32[1,128,512]{1,2,0:T(8,128)} async-done(((f32[16,128,512]{1,2,0:T(8,128)}), f32[1,128,512]{1,2,0:T(8,128)}) %reduce-scatter.28.cloned.1.call-update) | async-done | bytes 262160
  539.7 2.0 bitcast_dynamic-update-slice_fusion.2
  545.3 2.2 constant_dynamic-update-slice_fusion.17
  547.6 2.1 constant_dynamic-update-slice_fusion.16
  549.7 2.0 constant_dynamic-update-slice_fusion.15
  551.7 2.1 constant_dynamic-update-slice_fusion.14
  553.8 10.4 %all-gather.23.cloned.1.call-done = bf16[1024,512]{1,0:T(8,128)(2,1)} async-done(((bf16[128,512]{1,0:T(8,128)(2,1)}), bf16[1024,512]{1,0:T(8,128)(2,1)}) %all-gather.23.cloned.1.call-update) | async-done | bytes 1048592 | tf_op jit(solution)/shard_map/all_gather | solution.py:8
  564.1 3.4 constant_dynamic-update-slice_fusion.13
  567.6 8.0 gather_fusion.4
  575.6 12.0 %copy.118 = bf16[64,128,512]{1,2,0:T(8,128)(2,1)} copy(bf16[64,128,512]{2,1,0:T(8,128)(2,1)} %gather_fusion.4) | data formatting | bytes 16777216 | tf_op jit(solution)/shard_map/jit(_take)/gather | solution.py:18
  587.6 8.4 fusion.40
  596.2 78.6 %reduce-scatter.30.cloned.1.call-done = f32[1,128,512]{1,2,0:T(8,128)} async-done(((f32[16,128,512]{1,2,0:T(8,128)}), f32[1,128,512]{1,2,0:T(8,128)}) %reduce-scatter.30.cloned.1.call-update) | async-done | bytes 262160
  677.1 22.0 %all-gather.25.cloned.1.call-done = bf16[1024,512]{1,0:T(8,128)(2,1)} async-done(((bf16[128,512]{1,0:T(8,128)(2,1)}), bf16[1024,512]{1,0:T(8,128)(2,1)}) %all-gather.25.cloned.1.call-update) | async-done | bytes 1048592 | tf_op jit(solution)/shard_map/all_gather | solution.py:8
  699.1 2.8 constant_dynamic-update-slice_fusion.12
  701.8 8.3 gather_fusion.5
  710.2 11.9 %copy.124 = bf16[64,128,512]{1,2,0:T(8,128)(2,1)} copy(bf16[64,128,512]{2,1,0:T(8,128)(2,1)} %gather_fusion.5) | data formatting | bytes 16777216 | tf_op jit(solution)/shard_map/jit(_take)/gather | solution.py:18
  722.1 8.3 fusion.43
  730.6 78.6 %reduce-scatter.32.cloned.1.call-done = f32[1,128,512]{1,2,0:T(8,128)} async-done(((f32[16,128,512]{1,2,0:T(8,128)}), f32[1,128,512]{1,2,0:T(8,128)}) %reduce-scatter.32.cloned.1.call-update) | async-done | bytes 262160
  809.3 1.9 bitcast_dynamic-update-slice_fusion
  811.5 22.1 %all-gather.27.cloned.1.call-done = bf16[1024,512]{1,0:T(8,128)(2,1)} async-done(((bf16[128,512]{1,0:T(8,128)(2,1)}), bf16[1024,512]{1,0:T(8,128)(2,1)}) %all-gather.27.cloned.1.call-update) | async-done | bytes 1048592 | tf_op jit(solution)/shard_map/all_gather | solution.py:8
  833.6 2.3 constant_dynamic-update-slice_fusion.11
  835.9 8.7 gather_fusion.6
  844.5 11.9 %copy.130 = bf16[64,128,512]{1,2,0:T(8,128)(2,1)} copy(bf16[64,128,512]{2,1,0:T(8,128)(2,1)} %gather_fusion.6) | data formatting | bytes 16777216 | tf_op jit(solution)/shard_map/jit(_take)/gather | solution.py:18
  856.5 8.3 fusion.46
  864.9 78.6 %reduce-scatter.34.cloned.1.call-done = f32[1,128,512]{1,2,0:T(8,128)} async-done(((f32[16,128,512]{1,2,0:T(8,128)}), f32[1,128,512]{1,2,0:T(8,128)}) %reduce-scatter.34.cloned.1.call-update) | async-done | bytes 262160
  (94 shorter events, 26.2 us)
Async XLA Ops:
  6.5 28.2 %all-gather.15.cloned.1.call-start = ((), (), s32[]{:S(2)}) async-start(), calls=%async_computation.7 | async-start | bytes 1179648 | tf_op jit(solution)/shard_map/all_gather | solution.py:8
  8.4 132.4 %reduce-scatter.22.cloned.1.call-start = ((), (), s32[]{:S(2)}) async-start(), calls=%async_computation.14 | async-start | bytes 4456448
  53.5 8.6 copy-start.4
  62.0 103.1 %copy-start = (bf16[1024,512]{1,0:T(8,128)(2,1)S(1)}, bf16[1024,512]{1,0:T(8,128)(2,1)}, u32[]{:S(2)}) copy-start(bf16[1024,512]{1,0:T(8,128)(2,1)} %all-gather.15.cloned.1.call-done) | copy-start | bytes 3145732
  62.1 103.1 %all-gather.17.cloned.1.call-start = ((), (), s32[]{:S(2)}) async-start(), calls=%async_computation.8 | async-start | bytes 1179648 | tf_op jit(solution)/shard_map/all_gather | solution.py:8
  142.7 128.6 %reduce-scatter.24.cloned.1.call-start = ((), (), s32[]{:S(2)}) async-start(), calls=%async_computation.15 | async-start | bytes 4456448
  172.1 12.0 %copy-start.10 = (pred[16,4]{1,0:T(8,128)(4,1)S(1)}, pred[16,4]{1,0:T(8,128)(4,1)}, u32[]{:S(2)}) copy-start(pred[16,4]{1,0:T(8,128)(4,1)} %copy.98) | copy-start | bytes 196
  184.1 8.6 copy-start.5
  184.1 89.3 %copy-start.8 = (pred[16,4]{0,1:T(4,128)(4,1)S(1)}, pred[16,4]{0,1:T(4,128)(4,1)}, u32[]{:S(2)}) copy-start(pred[16,4]{0,1:T(4,128)(4,1)} %get-tuple-element.32) | copy-start | bytes 196
  184.1 111.6 %copy-start.1 = (bf16[1024,512]{1,0:T(8,128)(2,1)S(1)}, bf16[1024,512]{1,0:T(8,128)(2,1)}, u32[]{:S(2)}) copy-start(bf16[1024,512]{1,0:T(8,128)(2,1)} %all-gather.17.cloned.1.call-done) | copy-start | bytes 3145732
  192.6 103.0 %all-gather.19.cloned.1.call-start = ((), (), s32[]{:S(2)}) async-start(), calls=%async_computation.9 | async-start | bytes 1179648 | tf_op jit(solution)/shard_map/all_gather | solution.py:8
  273.2 132.0 %reduce-scatter.26.cloned.1.call-start = ((), (), s32[]{:S(2)}) async-start(), calls=%async_computation.16 | async-start | bytes 4456448
  305.9 12.0 %copy-start.11 = (pred[16,4]{1,0:T(8,128)(4,1)S(1)}, pred[16,4]{1,0:T(8,128)(4,1)}, u32[]{:S(2)}) copy-start(pred[16,4]{1,0:T(8,128)(4,1)} %copy.104) | copy-start | bytes 196
  317.9 111.7 %copy-start.2 = (bf16[1024,512]{1,0:T(8,128)(2,1)S(1)}, bf16[1024,512]{1,0:T(8,128)(2,1)}, u32[]{:S(2)}) copy-start(bf16[1024,512]{1,0:T(8,128)(2,1)} %all-gather.19.cloned.1.call-done) | copy-start | bytes 3145732
  326.5 103.1 %all-gather.21.cloned.1.call-start = ((), (), s32[]{:S(2)}) async-start(), calls=%async_computation.10 | async-start | bytes 1179648 | tf_op jit(solution)/shard_map/all_gather | solution.py:8
  407.2 132.6 %reduce-scatter.28.cloned.1.call-start = ((), (), s32[]{:S(2)}) async-start(), calls=%async_computation.17 | async-start | bytes 4456448
  461.0 103.1 %all-gather.23.cloned.1.call-start = ((), (), s32[]{:S(2)}) async-start(), calls=%async_computation.11 | async-start | bytes 1179648 | tf_op jit(solution)/shard_map/all_gather | solution.py:8
  541.7 133.1 %reduce-scatter.30.cloned.1.call-start = ((), (), s32[]{:S(2)}) async-start(), calls=%async_computation.18 | async-start | bytes 4456448
  545.3 6.4 copy-start.3
  575.6 12.0 %copy-start.9 = (pred[16,4]{1,0:T(8,128)(4,1)S(1)}, pred[16,4]{1,0:T(8,128)(4,1)}, u32[]{:S(2)}) copy-start(pred[16,4]{1,0:T(8,128)(4,1)} %copy.116) | copy-start | bytes 196
  587.6 89.4 %copy-start.7 = (pred[16,4]{0,1:T(4,128)(4,1)S(1)}, pred[16,4]{0,1:T(4,128)(4,1)}, u32[]{:S(2)}) copy-start(pred[16,4]{0,1:T(4,128)(4,1)} %get-tuple-element.35) | copy-start | bytes 196
  596.0 103.1 %all-gather.25.cloned.1.call-start = ((), (), s32[]{:S(2)}) async-start(), calls=%async_computation.12 | async-start | bytes 1179648 | tf_op jit(solution)/shard_map/all_gather | solution.py:8
  676.7 132.6 %reduce-scatter.32.cloned.1.call-start = ((), (), s32[]{:S(2)}) async-start(), calls=%async_computation.19 | async-start | bytes 4456448
  722.1 89.3 %copy-start.6 = (pred[16,4]{0,1:T(4,128)(4,1)S(1)}, pred[16,4]{0,1:T(4,128)(4,1)}, u32[]{:S(2)}) copy-start(pred[16,4]{0,1:T(4,128)(4,1)} %get-tuple-element.29) | copy-start | bytes 196
  730.5 103.1 %all-gather.27.cloned.1.call-start = ((), (), s32[]{:S(2)}) async-start(), calls=%async_computation.13 | async-start | bytes 1179648 | tf_op jit(solution)/shard_map/all_gather | solution.py:8
  811.2 132.4 %reduce-scatter.34.cloned.1.call-start = ((), (), s32[]{:S(2)}) async-start(), calls=%async_computation.20 | async-start | bytes 4456448
Sparse Core Ops, SparseCore 0:
  9.0 25.6 all-gather.14
  62.2 78.5 reduce-scatter.21
  142.8 22.2 all-gather.16
  192.8 78.4 reduce-scatter.23
  273.3 22.2 all-gather.18
  326.6 78.5 reduce-scatter.25
  407.3 22.2 all-gather.20
  461.1 78.5 reduce-scatter.27
  541.8 22.2 all-gather.22
  596.1 78.6 reduce-scatter.29
  676.8 22.2 all-gather.24
  730.6 78.6 reduce-scatter.31
  811.3 22.2 all-gather.26
  864.9 78.6 reduce-scatter.33
where the time goes:
time: 955 us; the launch traced here: 952 us
  waiting for transfers between devices  687 us (72%)
  local copies, waits for them, and re-layouts  165 us (17%)
  matrix products  74.1 us (8%)
  between operations  13.4 us (1%)
  other arithmetic  11.7 us (1%)
    unnamed x21, waiting for transfers between devices  546 us
    all_gather x7, waiting for transfers between devices, broadcast_solved(): return lax.all_gather(solved_block[None], 'col', axis=0, tiled=True)  140 us
    gather x14, local copies, waits for them, and re-layouts, contribute(): picked = jnp.take(source_pool, source_ids, axis=0)  136 us
    dot_general x7, matrix products, contribute(): jnp.einsum('tkab,tkbn->tan', blocks, picked, preferred_element_type=jnp.f...  58.9 us
  transfers between devices with their start and end apart: 14, of which 14 were waited for; matrix products, arithmetic and copies ran while one was open for 3% of the time, Pallas kernels for 0%

commit v1 on v0

--- a/solution.py
+++ b/solution.py
@@ -5,7 +5,13 @@
 
 
 def broadcast_solved(solved_block):
-    return lax.all_gather(solved_block[None], "col", axis=0, tiled=True)
+
+    def note_turns(obj):
+        top = jnp.stack(tuple((obj for _ in range(lax.axis_size("col")))))
+        everything = lax.all_to_all(top, axis_name="col", split_axis=0, concat_axis=0)
+        return jnp.concatenate(everything, axis=0)
+
+    return note_turns(solved_block[None])
 
 
 def reduce_updates(update_term):

time: 955 us -> 924 us (0.968)
  waiting for transfers between devices: 687 us -> 620 us
  starting transfers between devices: 0.95 us -> 30.8 us
    all_gather x7 -> x0, waiting for transfers between devices: 140 us -> none  [broadcast_solved(): return lax.all_gather(solved_block[None], 'col', axis=0, tiled=True)]
    all_to_all x0 -> x7, waiting for transfers between devices: none -> 93.2 us  [note_turns(): lax.all_to_all(top, axis_name='col', split_axis=0, concat_axis=0)]
    all_to_all x0 -> x7, starting transfers between devices: none -> 29.9 us  [note_turns(): lax.all_to_all(top, axis_name='col', split_axis=0, concat_axis=0)]
    unnamed x21 -> x14, waiting for transfers between devices: 546 us -> 527 us
where the time goes in v1:
time: 924 us; the launch traced here: 921 us
  waiting for transfers between devices  620 us (67%)
  local copies, waits for them, and re-layouts  172 us (19%)
  matrix products  73.4 us (8%)
  starting transfers between devices  30.8 us (3%)
  between operations  13.6 us (1%)
  other arithmetic  11.3 us (1%)
    unnamed x14, waiting for transfers between devices  527 us
    gather x14, local copies, waits for them, and re-layouts, contribute(): picked = jnp.take(source_pool, source_ids, axis=0)  137 us
    all_to_all x7, waiting for transfers between devices, note_turns(): lax.all_to_all(top, axis_name='col', split_axis=0, concat_axis=0)  93.2 us
    dot_general x7, matrix products, contribute(): jnp.einsum('tkab,tkbn->tan', blocks, picked, preferred_element_type=jnp.f...  58.5 us
    all_to_all x7, starting transfers between devices, note_turns(): lax.all_to_all(top, axis_name='col', split_axis=0, concat_axis=0)  29.9 us
  transfers between devices with their start and end apart: 14, of which 14 were waited for; matrix products, arithmetic and copies ran while one was open for 3% of the time, Pallas kernels for 0%

profile of v1, /device:TPU:0, one launch (start us, length us, event | category | flops | bytes accessed | tf_op | source)
XLA Modules:
  0.0 921.2 jit_solution(5509230085931677026)
XLA Ops:
  9.4 4.4 all-to-all-start
  16.9 12.8 %all-to-all-done = bf16[8,1,128,512]{3,2,1,0:T(8,128)(2,1)S(1)} async-done(((bf16[8,1,128,512]{3,2,1,0:T(8,128)(2,1)}), bf16[8,1,128,512]{3,2,1,0:T(8,128)(2,1)S(1)}, u32[]{:S(2)}, u32[]{:S(2)}) %all-to-all-start) | async-done | bytes 1048608 | tf_op jit(solution)/shard_map/all_to_all | solution.py:11
  29.7 5.5 gather_fusion
  35.3 12.2 %copy.87 = bf16[16,4,128,512]{2,3,1,0:T(8,128)(2,1)} copy(bf16[16,4,128,512]{3,2,1,0:T(8,128)(2,1)} %bitcast.339) | data formatting | bytes 16777216 | tf_op jit(solution)/shard_map/jit(_take)/gather | solution.py:24
  47.5 8.4 fusion.28
  56.9 78.4 %reduce-scatter.22.cloned.1.call-done = f32[1,128,512]{1,2,0:T(8,128)} async-done(((f32[16,128,512]{1,2,0:T(8,128)}), f32[1,128,512]{1,2,0:T(8,128)}) %reduce-scatter.22.cloned.1.call-update) | async-done | bytes 262160
  138.3 4.3 all-to-all-start.1
  143.4 15.0 %all-to-all-done.1 = bf16[8,1,128,512]{3,2,1,0:T(8,128)(2,1)S(1)} async-done(((bf16[8,1,128,512]{3,2,1,0:T(8,128)(2,1)}), bf16[8,1,128,512]{3,2,1,0:T(8,128)(2,1)S(1)}, u32[]{:S(2)}, u32[]{:S(2)}) %all-to-all-start.1) | async-done | bytes 1048608 | tf_op jit(solution)/shard_map/all_to_all | solution.py:11
  160.8 5.5 gather_fusion.1
  166.4 12.2 %copy.93 = bf16[16,4,128,512]{2,3,1,0:T(8,128)(2,1)} copy(bf16[16,4,128,512]{3,2,1,0:T(8,128)(2,1)} %bitcast.333) | data formatting | bytes 16777216 | tf_op jit(solution)/shard_map/jit(_take)/gather | solution.py:24
  178.6 8.4 fusion.31
  187.2 76.0 %reduce-scatter.24.cloned.1.call-done = f32[1,128,512]{1,2,0:T(8,128)} async-done(((f32[16,128,512]{1,2,0:T(8,128)}), f32[1,128,512]{1,2,0:T(8,128)}) %reduce-scatter.24.cloned.1.call-update) | async-done | bytes 262160
  266.1 4.3 all-to-all-start.2
  273.3 13.0 %all-to-all-done.2 = bf16[8,1,128,512]{3,2,1,0:T(8,128)(2,1)S(1)} async-done(((bf16[8,1,128,512]{3,2,1,0:T(8,128)(2,1)}), bf16[8,1,128,512]{3,2,1,0:T(8,128)(2,1)S(1)}, u32[]{:S(2)}, u32[]{:S(2)}) %all-to-all-start.2) | async-done | bytes 1048608 | tf_op jit(solution)/shard_map/all_to_all | solution.py:11
  288.1 7.4 gather_fusion.2
  295.6 12.2 %copy.99 = bf16[16,4,128,512]{2,3,1,0:T(8,128)(2,1)} copy(bf16[16,4,128,512]{3,2,1,0:T(8,128)(2,1)} %bitcast.334) | data formatting | bytes 16777216 | tf_op jit(solution)/shard_map/jit(_take)/gather | solution.py:24
  307.8 8.3 fusion.34
  317.8 74.5 %reduce-scatter.26.cloned.1.call-done = f32[1,128,512]{1,2,0:T(8,128)} async-done(((f32[16,128,512]{1,2,0:T(8,128)}), f32[1,128,512]{1,2,0:T(8,128)}) %reduce-scatter.26.cloned.1.call-update) | async-done | bytes 262160
  395.3 4.2 all-to-all-start.3
  402.4 13.1 %all-to-all-done.3 = bf16[8,1,128,512]{3,2,1,0:T(8,128)(2,1)} async-done(((bf16[8,1,128,512]{3,2,1,0:T(8,128)(2,1)}), bf16[8,1,128,512]{3,2,1,0:T(8,128)(2,1)}, u32[]{:S(2)}, u32[]{:S(2)}) %all-to-all-start.3) | async-done | bytes 1048608 | tf_op jit(solution)/shard_map/all_to_all | solution.py:11
  415.6 3.3 pad_maximum_fusion
  418.9 7.8 gather_fusion.3
  426.7 12.2 %copy.105 = bf16[16,4,128,512]{2,3,1,0:T(8,128)(2,1)} copy(bf16[16,4,128,512]{3,2,1,0:T(8,128)(2,1)} %bitcast.335) | data formatting | bytes 16777216 | tf_op jit(solution)/shard_map/jit(_take)/gather | solution.py:24
  438.9 8.3 fusion.37
  451.6 2.1 constant_dynamic-update-slice_fusion.11
  453.6 69.7 %reduce-scatter.28.cloned.1.call-done = f32[1,128,512]{1,2,0:T(8,128)} async-done(((f32[16,128,512]{1,2,0:T(8,128)}), f32[1,128,512]{1,2,0:T(8,128)}) %reduce-scatter.28.cloned.1.call-update) | async-done | bytes 262160
  526.4 4.2 all-to-all-start.4
  530.9 2.1 constant_dynamic-update-slice_fusion.10
  532.9 2.0 constant_dynamic-update-slice_fusion.9
  534.9 3.3 constant_dynamic-update-slice_fusion.8
  538.2 8.3 all-to-all-done.4
  546.5 2.0 bitcast_dynamic-update-slice_fusion.3
  548.5 8.0 gather_fusion.4
  556.6 12.2 %copy.111 = bf16[16,4,128,512]{2,3,1,0:T(8,128)(2,1)} copy(bf16[16,4,128,512]{3,2,1,0:T(8,128)(2,1)} %bitcast.336) | data formatting | bytes 16777216 | tf_op jit(solution)/shard_map/jit(_take)/gather | solution.py:24
  568.8 8.3 fusion.40
  577.3 76.1 %reduce-scatter.30.cloned.1.call-done = f32[1,128,512]{1,2,0:T(8,128)} async-done(((f32[16,128,512]{1,2,0:T(8,128)}), f32[1,128,512]{1,2,0:T(8,128)}) %reduce-scatter.30.cloned.1.call-update) | async-done | bytes 262160
  656.3 4.3 all-to-all-start.5
  660.9 15.6 %all-to-all-done.5 = bf16[8,1,128,512]{3,2,1,0:T(8,128)(2,1)S(1)} async-done(((bf16[8,1,128,512]{3,2,1,0:T(8,128)(2,1)}), bf16[8,1,128,512]{3,2,1,0:T(8,128)(2,1)S(1)}, u32[]{:S(2)}, u32[]{:S(2)}) %all-to-all-start.5) | async-done | bytes 1048608 | tf_op jit(solution)/shard_map/all_to_all | solution.py:11
  678.0 8.3 gather_fusion.5
  686.4 12.2 %copy.117 = bf16[16,4,128,512]{2,3,1,0:T(8,128)(2,1)} copy(bf16[16,4,128,512]{3,2,1,0:T(8,128)(2,1)} %bitcast.337) | data formatting | bytes 16777216 | tf_op jit(solution)/shard_map/jit(_take)/gather | solution.py:24
  698.6 8.3 fusion.43
  707.1 76.0 %reduce-scatter.32.cloned.1.call-done = f32[1,128,512]{1,2,0:T(8,128)} async-done(((f32[16,128,512]{1,2,0:T(8,128)}), f32[1,128,512]{1,2,0:T(8,128)}) %reduce-scatter.32.cloned.1.call-update) | async-done | bytes 262160
  786.0 4.2 all-to-all-start.6
  790.9 15.3 %all-to-all-done.6 = bf16[8,1,128,512]{3,2,1,0:T(8,128)(2,1)S(1)} async-done(((bf16[8,1,128,512]{3,2,1,0:T(8,128)(2,1)}), bf16[8,1,128,512]{3,2,1,0:T(8,128)(2,1)S(1)}, u32[]{:S(2)}, u32[]{:S(2)}) %all-to-all-start.6) | async-done | bytes 1048608 | tf_op jit(solution)/shard_map/all_to_all | solution.py:11
  807.2 8.6 gather_fusion.6
  815.9 12.2 %copy.123 = bf16[16,4,128,512]{2,3,1,0:T(8,128)(2,1)} copy(bf16[16,4,128,512]{3,2,1,0:T(8,128)(2,1)} %bitcast.338) | data formatting | bytes 16777216 | tf_op jit(solution)/shard_map/jit(_take)/gather | solution.py:24
  828.1 8.3 fusion.46
  836.6 75.9 %reduce-scatter.34.cloned.1.call-done = f32[1,128,512]{1,2,0:T(8,128)} async-done(((f32[16,128,512]{1,2,0:T(8,128)}), f32[1,128,512]{1,2,0:T(8,128)}) %reduce-scatter.34.cloned.1.call-update) | async-done | bytes 262160
  (85 shorter events, 47.5 us)
Async XLA Ops:
  9.4 20.3 %all-to-all-start = ((bf16[8,1,128,512]{3,2,1,0:T(8,128)(2,1)}), bf16[8,1,128,512]{3,2,1,0:T(8,128)(2,1)S(1)}, u32[]{:S(2)}, u32[]{:S(2)}) async-start(bf16[8,1,128,512]{3,2,1,0:T(8,128)(2,1)} %stack.49), calls=%async_computation | async-start | bytes 2097152 | tf_op jit(solution)/shard_map/all_to_all | solution.py:11
  13.8 121.5 %reduce-scatter.22.cloned.1.call-start = ((), (), s32[]{:S(2)}) async-start(), calls=%async_computation.14 | async-start | bytes 4456448
  47.5 8.5 copy-start.2
  138.3 20.2 %all-to-all-start.1 = ((bf16[8,1,128,512]{3,2,1,0:T(8,128)(2,1)}), bf16[8,1,128,512]{3,2,1,0:T(8,128)(2,1)S(1)}, u32[]{:S(2)}, u32[]{:S(2)}) async-start(bf16[8,1,128,512]{3,2,1,0:T(8,128)(2,1)} %stack.51), calls=%async_computation.1 | async-start | bytes 2097152 | tf_op jit(solution)/shard_map/all_to_all | solution.py:11
  142.5 120.6 %reduce-scatter.24.cloned.1.call-start = ((), (), s32[]{:S(2)}) async-start(), calls=%async_computation.15 | async-start | bytes 4456448
  158.4 1.0 copy-start
  166.4 12.3 %copy-start.6 = (pred[16,4]{1,0:T(8,128)(4,1)S(1)}, pred[16,4]{1,0:T(8,128)(4,1)}, u32[]{:S(2)}) copy-start(pred[16,4]{1,0:T(8,128)(4,1)} %copy.91) | copy-start | bytes 196
  178.6 8.4 copy-start.3
  187.0 99.3 %copy-start.1 = (bf16[8,1,128,512]{3,2,1,0:T(8,128)(2,1)S(1)}, bf16[8,1,128,512]{3,2,1,0:T(8,128)(2,1)}, u32[]{:S(2)}) copy-start(bf16[8,1,128,512]{3,2,1,0:T(8,128)(2,1)} %copy-done) | copy-start | bytes 3145732
  266.1 20.2 %all-to-all-start.2 = ((bf16[8,1,128,512]{3,2,1,0:T(8,128)(2,1)}), bf16[8,1,128,512]{3,2,1,0:T(8,128)(2,1)S(1)}, u32[]{:S(2)}, u32[]{:S(2)}) async-start(bf16[8,1,128,512]{3,2,1,0:T(8,128)(2,1)} %stack.53), calls=%async_computation.2 | async-start | bytes 2097152 | tf_op jit(solution)/shard_map/all_to_all | solution.py:11
  270.3 122.0 %reduce-scatter.26.cloned.1.call-start = ((), (), s32[]{:S(2)}) async-start(), calls=%async_computation.16 | async-start | bytes 4456448
  395.3 20.3 %all-to-all-start.3 = ((bf16[8,1,128,512]{3,2,1,0:T(8,128)(2,1)}), bf16[8,1,128,512]{3,2,1,0:T(8,128)(2,1)}, u32[]{:S(2)}, u32[]{:S(2)}) async-start(bf16[8,1,128,512]{3,2,1,0:T(8,128)(2,1)} %stack.55), calls=%async_computation.3 | async-start | bytes 2097152 | tf_op jit(solution)/shard_map/all_to_all | solution.py:11
  399.6 123.8 %reduce-scatter.28.cloned.1.call-start = ((), (), s32[]{:S(2)}) async-start(), calls=%async_computation.17 | async-start | bytes 4456448
  526.4 20.2 %all-to-all-start.4 = ((bf16[8,1,128,512]{3,2,1,0:T(8,128)(2,1)}), bf16[8,1,128,512]{3,2,1,0:T(8,128)(2,1)S(1)}, u32[]{:S(2)}, u32[]{:S(2)}) async-start(bf16[8,1,128,512]{3,2,1,0:T(8,128)(2,1)} %stack.57), calls=%async_computation.4 | async-start | bytes 2097152 | tf_op jit(solution)/shard_map/all_to_all | solution.py:11
  530.6 122.8 %reduce-scatter.30.cloned.1.call-start = ((), (), s32[]{:S(2)}) async-start(), calls=%async_computation.18 | async-start | bytes 4456448
  577.2 83.6 %copy-start.5 = (pred[16,4]{0,1:T(4,128)(4,1)S(1)}, pred[16,4]{0,1:T(4,128)(4,1)}, u32[]{:S(2)}) copy-start(pred[16,4]{0,1:T(4,128)(4,1)} %get-tuple-element.35) | copy-start | bytes 196
  656.3 20.2 %all-to-all-start.5 = ((bf16[8,1,128,512]{3,2,1,0:T(8,128)(2,1)}), bf16[8,1,128,512]{3,2,1,0:T(8,128)(2,1)S(1)}, u32[]{:S(2)}, u32[]{:S(2)}) async-start(bf16[8,1,128,512]{3,2,1,0:T(8,128)(2,1)} %stack.59), calls=%async_computation.5 | async-start | bytes 2097152 | tf_op jit(solution)/shard_map/all_to_all | solution.py:11
  660.6 122.6 %reduce-scatter.32.cloned.1.call-start = ((), (), s32[]{:S(2)}) async-start(), calls=%async_computation.19 | async-start | bytes 4456448
  706.9 83.8 %copy-start.4 = (pred[16,4]{0,1:T(4,128)(4,1)S(1)}, pred[16,4]{0,1:T(4,128)(4,1)}, u32[]{:S(2)}) copy-start(pred[16,4]{0,1:T(4,128)(4,1)} %get-tuple-element.29) | copy-start | bytes 196
  786.0 20.2 %all-to-all-start.6 = ((bf16[8,1,128,512]{3,2,1,0:T(8,128)(2,1)}), bf16[8,1,128,512]{3,2,1,0:T(8,128)(2,1)S(1)}, u32[]{:S(2)}, u32[]{:S(2)}) async-start(bf16[8,1,128,512]{3,2,1,0:T(8,128)(2,1)} %stack.61), calls=%async_computation.6 | async-start | bytes 2097152 | tf_op jit(solution)/shard_map/all_to_all | solution.py:11
  790.3 122.3 %reduce-scatter.34.cloned.1.call-start = ((), (), s32[]{:S(2)}) async-start(), calls=%async_computation.20 | async-start | bytes 4456448
Sparse Core Ops, SparseCore 0:
  56.1 79.1 reduce-scatter.21
  187.2 75.9 reduce-scatter.23
  316.3 75.9 reduce-scatter.25
  447.4 75.9 reduce-scatter.27
  577.3 76.0 reduce-scatter.29
  707.1 75.9 reduce-scatter.31
  836.6 75.8 reduce-scatter.33
